TPU v7x, 256 devices: a whole 4x4x8 slice. The times are simulated.
256 devices in a mesh: prow: 32 (over y, z), pcol: 8 (over x, core).
Axes of the slice: x: 4, y: 4, z: 8, core: 2. Of those that a mesh axis runs over, the one named last changes fastest.
Arguments:
- panel_rows: float32 [2, 1024, 98304], P(None, None, ('prow', 'pcol')), may hold values from -0.078125 to 0.078125
- solved: float32 [98304, 1024], P(('prow', 'pcol')), may hold values from -6 to 6
- right_side: float32 [2, 1024, 1024], P(None, 'prow', 'pcol'), may hold values from -6 to 6
- coupling: float32 [1024, 1024], P(None, 'prow'), may hold values from -0.1875 to 0.1875
- inverses: float32 [2, 1024, 1024], P(None, 'prow'), may hold values from -2 to 2, as said below
Outputs:
- panels: float32 [2, 1024, 1024], P(None, 'prow', 'pcol')
Inputs may be any that keep to these rules, and one draw needn't show every extreme that they name: `inverses`: each tile is zero above its diagonal, and its diagonal entries are positive.
All inputs are finite; a program needn't handle non-finite values.
Results may differ from a plain program's by a relative error of at most 0.000088.
Values sent between devices are 32-bit elements; how exact they have to be, the bound alone decides.
No kernel may reach another device: no remote copies, remote signals or barrier semaphores. Data moves between devices by JAX's collectives and lax.ppermute only.
A program may use at most 64 MiB of HBM per device.

v0:
```python
import jax
import jax.numpy as jnp
from jax import lax
from jax.sharding import PartitionSpec as P


def combine_old(partial_value):
    by_rows = lax.psum_scatter(partial_value, "prow", scatter_dimension=1, tiled=True)
    return lax.psum_scatter(by_rows, "pcol", scatter_dimension=2, tiled=True)


def apply_inverse(inverse_rows, residue):
    highest = lax.Precision.HIGHEST
    return jnp.dot(
        inverse_rows,
        lax.all_gather(residue, "prow", axis=0, tiled=True),
        precision=highest,
        preferred_element_type=jnp.float32,
    )


def body(panel_rows, solved, right_side, coupling, inverses):
    highest = lax.Precision.HIGHEST
    tile_rows = panel_rows.shape[1]
    solved_rows = panel_rows.shape[2]
    flat_rows = panel_rows.reshape(2 * tile_rows, solved_rows)
    partial_value = jnp.dot(
        flat_rows, solved, precision=highest, preferred_element_type=jnp.float32
    )
    partial_value = partial_value.reshape(2, tile_rows, solved.shape[1])
    reduced = combine_old(partial_value)
    first_panel = apply_inverse(inverses[0], right_side[0] - reduced[0])
    coupling_term = jnp.dot(
        coupling, first_panel, precision=highest, preferred_element_type=jnp.float32
    )
    coupling_part = lax.psum_scatter(coupling_term, "prow", scatter_dimension=0, tiled=True)
    second_rest = right_side[1] - reduced[1] - coupling_part
    second_panel = apply_inverse(inverses[1], second_rest)
    return jnp.stack([first_panel, second_panel])


def solution(mesh):
    return jax.shard_map(
        body,
        mesh=mesh,
        in_specs=(
            P(None, None, ("prow", "pcol")),
            P(("prow", "pcol"), None),
            P(None, "prow", "pcol"),
            P(None, "prow"),
            P(None, "prow", None),
        ),
        out_specs=P(None, "prow", "pcol"),
        check_vma=False,
    )
```

profile of v0, /device:TPU:2, one launch (start us, length us, event | category | flops | bytes accessed | tf_op | source)
XLA Modules:
  0.0 615.7 jit_solution(7814447639951448719)
XLA Ops:
  6.5 0.0 copy-start
  6.5 0.0 reduce-scatter.4.cloned.1.call-start
  6.5 1.9 copy-done
  8.4 16.8 %fusion = f32[2,1024,1024]{2,1,0:T(8,128)} fusion(f32[2,1024,384]{2,1,0:T(8,128)S(1)} %copy-done, f32[384,1024]{1,0:T(8,128)} %param.6), kind=kOutput, calls=%fused_computation | convolution fusion | flops 9663676416 | bytes 13107200 | tf_op jit(solution)/shard_map/dot_general | solution.py:27
  25.2 0.0 copy-start.1
  25.2 0.0 copy-start.2
  25.2 0.0 reduce-scatter.4.cloned.1.call-update
  25.2 0.0 reduce-scatter.6.cloned.1.call-start
  25.3 233.9 %reduce-scatter.4.cloned.1.call-done = f32[2,32,1024]{2,1,0:T(8,128)} async-done(((f32[2,1024,1024]{2,1,0:T(8,128)}), f32[2,32,1024]{2,1,0:T(8,128)}) %reduce-scatter.4.cloned.1.call-update) | async-done | bytes 262160 | tf_op jit(solution)/shard_map/reduce_scatter | solution.py:8
  259.2 0.0 reduce-scatter.6.cloned.1.call-update
  259.3 0.0 reduce-scatter.8.cloned.1.call-start
  259.3 31.3 %reduce-scatter.6.cloned.1.call-done = f32[2,32,128]{2,1,0:T(8,128)} async-done(((f32[2,32,1024]{2,1,0:T(8,128)}), f32[2,32,128]{2,1,0:T(8,128)}) %reduce-scatter.6.cloned.1.call-update) | async-done | bytes 32784 | tf_op jit(solution)/shard_map/reduce_scatter | solution.py:9
  290.6 0.7 slice_subtract_fusion.1
  291.4 50.4 %all-gather = f32[1,1024,128]{2,1,0:T(8,128)S(1)} all-gather(f32[1,32,128]{2,1,0:T(8,128)S(1)} %slice_subtract_fusion.1), channel_id=2, replica_groups=mesh['prow'=32,'pcol'=8] {'prow'}, dimensions={1}, use_global_device_ids=true | all-gather | bytes 540672 | tf_op jit(solution)/shard_map/all_gather | solution.py:16
  341.8 0.0 copy-done.1
  341.8 0.4 fusion.2
  342.2 0.0 copy-done.2
  342.2 1.8 convolution_bitcast_fusion
  344.0 0.0 reduce-scatter.8.cloned.1.call-update
  344.0 215.2 %reduce-scatter.8.cloned.1.call-done = f32[32,128]{1,0:T(8,128)} async-done(((f32[1024,128]{1,0:T(8,128)}), f32[32,128]{1,0:T(8,128)}) %reduce-scatter.8.cloned.1.call-update) | async-done | bytes 16400 | tf_op jit(solution)/shard_map/reduce_scatter | solution.py:36
  559.3 0.8 fusion.9
  560.0 48.1 %all_gather.7 = f32[1024,128]{1,0:T(8,128)S(1)} all-gather(f32[32,128]{1,0:T(8,128)S(1)} %fusion.9), channel_id=1, replica_groups=mesh['prow'=32,'pcol'=8] {'prow'}, dimensions={0}, use_global_device_ids=true | all-gather | bytes 540672 | tf_op jit(solution)/shard_map/all_gather | solution.py:16
  608.1 0.4 convolution_bitcast_fusion.1
  608.5 0.6 pad_maximum_fusion
Async XLA Ops:
  6.5 1.9 copy-start
  6.5 252.7 %reduce-scatter.4.cloned.1.call-start = ((), (), s32[]{:S(2)}) async-start(), calls=%async_computation.3 | async-start | bytes 8650752 | tf_op jit(solution)/shard_map/reduce_scatter | solution.py:8
  25.2 316.6 %copy-start.1 = (f32[2,32,1024]{2,1,0:T(8,128)S(1)}, f32[2,32,1024]{2,1,0:T(8,128)}, u32[]{:S(2)}) copy-start(f32[2,32,1024]{2,1,0:T(8,128)} %param.9) | copy-start | bytes 786436
  25.2 317.0 %copy-start.2 = (f32[1024,32]{0,1:T(8,128)S(1)}, f32[1024,32]{0,1:T(8,128)}, u32[]{:S(2)}) copy-start(f32[1024,32]{0,1:T(8,128)} %param.8) | copy-start | bytes 393220
  25.2 265.4 %reduce-scatter.6.cloned.1.call-start = ((), (), s32[]{:S(2)}) async-start(), calls=%async_computation.4 | async-start | bytes 294912 | tf_op jit(solution)/shard_map/reduce_scatter | solution.py:9
  259.3 300.0 %reduce-scatter.8.cloned.1.call-start = ((), (), s32[]{:S(2)}) async-start(), calls=%async_computation.5 | async-start | bytes 540672 | tf_op jit(solution)/shard_map/reduce_scatter | solution.py:36
Sparse Core Ops, SparseCore 0:
  25.4 233.8 reduce-scatter.3
  261.7 28.8 reduce-scatter.5
  344.2 215.0 reduce-scatter.7
where the time goes:
time: 616 us
  waiting for transfers between devices  481 us (78%)
  blocking collectives  98.5 us (16%)
  matrix products  19.4 us (3%)
  between operations  13.1 us (2%)
    reduce_scatter x1, waiting for transfers between devices, combine_old(): lax.psum_scatter(partial_value, 'prow', scatter_dimension=1, tiled=True)  234 us
    reduce_scatter x1, waiting for transfers between devices, body(): lax.psum_scatter(coupling_term, 'prow', scatter_dimension=0, tiled=True)  215 us
    all_gather x2, blocking collectives, apply_inverse(): lax.all_gather(residue, 'prow', axis=0, tiled=True)  98.5 us
    reduce_scatter x1, waiting for transfers between devices, combine_old(): return lax.psum_scatter(by_rows, 'pcol', scatter_dimension=2, tiled=True)  31.3 us
    dot_general x1, matrix products, body(): jnp.dot(flat_rows, solved, precision=highest, preferred_element_type=jnp....  16.8 us
  transfers between devices with their start and end apart: 3, of which 3 were waited for; matrix products, arithmetic and copies ran while one was open for 0% of the time, Pallas kernels for 0%

commit v1 on v0

--- a/solution.py
+++ b/solution.py
@@ -13,7 +13,9 @@
     highest = lax.Precision.HIGHEST
     return jnp.dot(
         inverse_rows,
-        lax.all_gather(residue, "prow", axis=0, tiled=True),
+        jnp.concatenate(
+            lax.all_to_all(jnp.stack([residue] * lax.axis_size("prow")), "prow", 0, 0), axis=0
+        ),
         precision=highest,
         preferred_element_type=jnp.float32,
     )

time: 616 us -> 564 us (0.916)
  blocking collectives: 98.5 us -> 45.2 us
    all_gather x2 -> x0, blocking collectives: 98.5 us -> none  [apply_inverse(): lax.all_gather(residue, 'prow', axis=0, tiled=True)]
    all_to_all x0 -> x2, blocking collectives: none -> 45.2 us  [apply_inverse(): lax.all_to_all(jnp.stack([residue] * lax.axis_size('prow')), 'prow', 0, 0)]
where the time goes in v1:
time: 564 us; the launch traced here: 563 us
  waiting for transfers between devices  481 us (85%)
  blocking collectives  45.2 us (8%)
  matrix products  19.4 us (3%)
  between operations  13.1 us (2%)
    reduce_scatter x1, waiting for transfers between devices, combine_old(): lax.psum_scatter(partial_value, 'prow', scatter_dimension=1, tiled=True)  234 us
    reduce_scatter x1, waiting for transfers between devices, body(): lax.psum_scatter(coupling_term, 'prow', scatter_dimension=0, tiled=True)  216 us
    all_to_all x2, blocking collectives, apply_inverse(): lax.all_to_all(jnp.stack([residue] * lax.axis_size('prow')), 'prow', 0, 0)  45.2 us
    reduce_scatter x1, waiting for transfers between devices, combine_old(): return lax.psum_scatter(by_rows, 'pcol', scatter_dimension=2, tiled=True)  31.3 us
    dot_general x1, matrix products, body(): jnp.dot(flat_rows, solved, precision=highest, preferred_element_type=jnp....  16.8 us
  transfers between devices with their start and end apart: 3, of which 3 were waited for; matrix products, arithmetic and copies ran while one was open for 0% of the time, Pallas kernels for 0%

profile of v1, /device:TPU:2, one launch (start us, length us, event | category | flops | bytes accessed | tf_op | source)
XLA Modules:
  0.0 562.8 jit_solution(39840252275019809)
XLA Ops:
  6.5 0.0 copy-start
  6.5 0.0 reduce-scatter.4.cloned.1.call-start
  6.5 1.9 copy-done
  8.4 16.8 %fusion = f32[2,1024,1024]{2,1,0:T(8,128)} fusion(f32[2,1024,384]{2,1,0:T(8,128)S(1)} %copy-done, f32[384,1024]{1,0:T(8,128)} %param.6), kind=kOutput, calls=%fused_computation | convolution fusion | flops 9663676416 | bytes 13107200 | tf_op jit(solution)/shard_map/dot_general | solution.py:29
  25.2 0.0 reduce-scatter.4.cloned.1.call-update
  25.2 0.0 reduce-scatter.6.cloned.1.call-start
  25.3 233.9 %reduce-scatter.4.cloned.1.call-done = f32[2,32,1024]{2,1,0:T(8,128)} async-done(((f32[2,1024,1024]{2,1,0:T(8,128)}), f32[2,32,1024]{2,1,0:T(8,128)}) %reduce-scatter.4.cloned.1.call-update) | async-done | bytes 262160 | tf_op jit(solution)/shard_map/reduce_scatter | solution.py:8
  259.2 0.0 reduce-scatter.6.cloned.1.call-update
  259.3 0.0 reduce-scatter.8.cloned.1.call-start
  259.3 31.3 %reduce-scatter.6.cloned.1.call-done = f32[2,32,128]{2,1,0:T(8,128)} async-done(((f32[2,32,1024]{2,1,0:T(8,128)}), f32[2,32,128]{2,1,0:T(8,128)}) %reduce-scatter.6.cloned.1.call-update) | async-done | bytes 32784 | tf_op jit(solution)/shard_map/reduce_scatter | solution.py:9
  290.6 0.7 fusion.9
  291.4 0.1 stack.13
  291.4 25.7 %all_to_all.10 = f32[32,32,128]{2,1,0:T(8,128)S(1)} all-to-all(f32[32,32,128]{2,1,0:T(8,128)S(1)} %stack.13), channel_id=1, replica_groups=mesh['prow'=32,'pcol'=8] {'prow'}, dimensions={0} | all-to-all | bytes 1048576 | tf_op jit(solution)/shard_map/all_to_all | solution.py:17
  317.1 0.0 copy-done.1
  317.1 0.4 fusion.3
  317.5 0.0 copy-done.2
  317.5 1.8 convolution_bitcast_fusion
  319.3 0.0 reduce-scatter.8.cloned.1.call-update
  319.3 215.5 %reduce-scatter.8.cloned.1.call-done = f32[32,128]{1,0:T(8,128)} async-done(((f32[1024,128]{1,0:T(8,128)}), f32[32,128]{1,0:T(8,128)}) %reduce-scatter.8.cloned.1.call-update) | async-done | bytes 16400 | tf_op jit(solution)/shard_map/reduce_scatter | solution.py:38
  534.9 0.8 fusion.8
  535.6 0.1 stack.15
  535.7 19.5 %all_to_all.11 = f32[32,32,128]{2,1,0:T(8,128)S(1)} all-to-all(f32[32,32,128]{2,1,0:T(8,128)S(1)} %stack.15), channel_id=1, replica_groups=mesh['prow'=32,'pcol'=8] {'prow'}, dimensions={0} | all-to-all | bytes 1048576 | tf_op jit(solution)/shard_map/all_to_all | solution.py:17
  555.2 0.4 convolution_bitcast_fusion.1
  555.6 0.6 pad_maximum_fusion
  (2 shorter events, 0.0 us)
Async XLA Ops:
  6.5 1.9 copy-start
  6.5 252.7 %reduce-scatter.4.cloned.1.call-start = ((), (), s32[]{:S(2)}) async-start(), calls=%async_computation.5 | async-start | bytes 8650752 | tf_op jit(solution)/shard_map/reduce_scatter | solution.py:8
  25.2 291.9 %copy-start.1 = (f32[2,32,1024]{2,1,0:T(8,128)S(1)}, f32[2,32,1024]{2,1,0:T(8,128)}, u32[]{:S(2)}) copy-start(f32[2,32,1024]{2,1,0:T(8,128)} %param.9) | copy-start | bytes 786436
  25.2 292.3 %copy-start.2 = (f32[1024,32]{0,1:T(8,128)S(1)}, f32[1024,32]{0,1:T(8,128)}, u32[]{:S(2)}) copy-start(f32[1024,32]{0,1:T(8,128)} %param.8) | copy-start | bytes 393220
  25.2 265.4 %reduce-scatter.6.cloned.1.call-start = ((), (), s32[]{:S(2)}) async-start(), calls=%async_computation.6 | async-start | bytes 294912 | tf_op jit(solution)/shard_map/reduce_scatter | solution.py:9
  259.3 275.6 %reduce-scatter.8.cloned.1.call-start = ((), (), s32[]{:S(2)}) async-start(), calls=%async_computation.7 | async-start | bytes 540672 | tf_op jit(solution)/shard_map/reduce_scatter | solution.py:38
Sparse Core Ops, SparseCore 0:
  25.4 233.8 reduce-scatter.3
  261.7 28.8 reduce-scatter.5
  319.5 215.3 reduce-scatter.7
